TPU v7x, 32 devices: a whole 2x2x4 slice. The times are simulated.
32 devices in a mesh: groups: 2 (over y), row: 8 (over z, core), col: 2 (over x).
Axes of the slice: x: 2, y: 2, z: 4, core: 2. Of those that a mesh axis runs over, the one named last changes fastest.
Arguments:
- nodes: bfloat16 [1024, 768], P(('groups', 'row')), parts along dimension 0, may hold values from -6 to 6
- chain_ids: int32 [1024], P(('groups', 'row')), parts along dimension 0, may hold values from 0 to 3, never falling along the last dimension, each value on 1 to 256 neighbouring positions
- residue_index: int32 [1024], P(('groups', 'row')), parts along dimension 0, may hold values from 0 to 63
- pad_mask: int32 [1024], P(('groups', 'row')), parts along dimension 0, may hold values from 0 to 1, as said below
- pairs: bfloat16 [64, 1024, 512], P(None, ('groups', 'row'), 'col'), parts along dimension 1, may hold values from -6 to 6
- node_gain: float32 [768], replicated, may hold values from 0.1 to 1.9
- w_qkv: bfloat16 [768, 2304], replicated, may hold values from -0.21875 to 0.21875
- w_out: bfloat16 [768, 768], replicated, may hold values from -0.4375 to 0.4375
- pair_gain: float32 [64], replicated, may hold values from 0.1 to 1.9
- w_bias_gate: bfloat16 [96, 64], replicated, may hold values from -0.75 to 0.75
- rel_table: float32 [48, 66], replicated, may hold values from -6 to 6
- w_edge: bfloat16 [64, 48], replicated, may hold values from -0.875 to 0.875
- edge_norm_gain: float32 [64], replicated, may hold values from 0.1 to 1.9
- w_mlp_in: bfloat16 [256, 64], replicated, may hold values from -0.75 to 0.75
- w_mlp_out: bfloat16 [64, 256], replicated, may hold values from -0.375 to 0.375
Outputs:
- node_update: bfloat16 [1024, 768], P(('groups', 'row')), parts along dimension 0
- pairs_out: bfloat16 [64, 1024, 512], P(None, ('groups', 'row'), 'col'), parts along dimension 1
There are 2 independent parts, one for each index of `groups`. A program takes and returns all parts, laid end to end along the dimension named above; an argument that names none is the same for every part. Nothing has to cross between parts.
Inputs may be any that keep to these rules, and one draw needn't show every extreme that they name: `chain_ids`: non-decreasing along the residues; each chain holds at most 256 residues. `pad_mask`: 1 on a leading run of at least 256 residues and 0 on the rest, which holds at least one residue.
All inputs are finite; a program needn't handle non-finite values.
Results may differ from a plain program's by a relative error of at most 0.0087.
Values may be sent and summed in bfloat16 or wider, within the bound.
A program may use at most 64 MiB of HBM per device.

v0:
```python
import jax
import jax.numpy as jnp
from jax import lax
from jax.sharding import PartitionSpec as P


def layer_norm(values, axis):
    mean = jnp.mean(values, axis=axis, keepdims=True)
    var = jnp.mean(jnp.square(values - mean), axis=axis, keepdims=True)
    return (values - mean) * lax.rsqrt(var + 1e-05)


def pair_block(
    zb,
    query_rows,
    key,
    value_rows,
    chain_r,
    res_r,
    chain_c,
    res_c,
    valid_c,
    pair_gain,
    w_bias_gate,
    rel_table,
    w_edge,
    edge_norm_gain,
    w_mlp_in,
    w_mlp_out,
):
    chans, nrow, ncol = zb.shape
    heads, classes_all = rel_table.shape
    zf = zb.astype(jnp.float32)
    pnorm = (layer_norm(zf, 0) * pair_gain[:, None, None]).astype(jnp.bfloat16)
    bias_gate = jnp.dot(
        w_bias_gate, pnorm.reshape(chans, nrow * ncol), preferred_element_type=jnp.float32
    ).reshape(2 * heads, nrow, ncol)
    bias = bias_gate[:heads]
    gate = bias_gate[heads:]
    offset_radius = (classes_all - 2) // 2
    offset = (
        jnp.clip(res_r[:, None] - res_c[None, :], -offset_radius, offset_radius) + offset_radius
    )
    offset_classes = jnp.where(
        chain_r[:, None] == chain_c[None, :], offset, 2 * offset_radius + 1
    ).astype(jnp.int32)
    class_ids = lax.broadcasted_iota(jnp.int32, (classes_all, nrow * ncol), 0)
    one_hot = (class_ids == offset_classes.reshape(1, nrow * ncol)).astype(jnp.float32)
    rel = jnp.dot(
        rel_table, one_hot, precision=lax.Precision.HIGHEST, preferred_element_type=jnp.float32
    ).reshape(heads, nrow, ncol)
    score_logits = jnp.einsum("axt,zxt->xaz", query_rows, key, preferred_element_type=jnp.float32)
    logits = jnp.clip(0.25 * score_logits + bias + rel, -5.0, 5.0)
    weights = jnp.where(valid_c[None, None, :], jnp.exp(logits), jnp.float32(0.0))
    gated_output = (weights * jax.nn.sigmoid(gate)).astype(jnp.bfloat16)
    numerator_rows = jnp.einsum(
        "qby,yqo->bqo", gated_output, value_rows, preferred_element_type=jnp.float32
    )
    denom = jnp.sum(weights, axis=2)
    edge = jnp.dot(
        w_edge,
        logits.astype(jnp.bfloat16).reshape(heads, nrow * ncol),
        preferred_element_type=jnp.float32,
    )
    first = zf.reshape(chans, nrow * ncol) + edge
    enorm = (layer_norm(first, 0) * edge_norm_gain[:, None]).astype(jnp.bfloat16)
    hidden = jax.nn.gelu(jnp.dot(w_mlp_in, enorm, preferred_element_type=jnp.float32)).astype(
        jnp.bfloat16
    )
    out = first + jnp.dot(w_mlp_out, hidden, preferred_element_type=jnp.float32)
    return (numerator_rows, denom, out.astype(jnp.bfloat16).reshape(chans, nrow, ncol))


def body(
    nodes,
    chain_ids,
    residue_index,
    pad_mask,
    pairs,
    node_gain,
    w_qkv,
    w_out,
    pair_gain,
    w_bias_gate,
    rel_table,
    w_edge,
    edge_norm_gain,
    w_mlp_in,
    w_mlp_out,
):
    rows, width = nodes.shape
    chans, _, cols = pairs.shape
    heads = rel_table.shape[0]
    head_size = width // heads
    col_start = lax.axis_index("col") * cols
    normed = (layer_norm(nodes.astype(jnp.float32), 1) * node_gain).astype(jnp.bfloat16)
    node_ints = jnp.stack([chain_ids, residue_index, pad_mask], axis=1)
    query_rows = jnp.dot(normed, w_qkv[:, :width], preferred_element_type=jnp.float32).astype(
        jnp.bfloat16
    )
    gathered, all_ints = (
        lax.all_gather(nodes, "row", axis=0, tiled=True),
        lax.all_gather(node_ints, "row", axis=0, tiled=True),
    )
    col_nodes = lax.dynamic_slice_in_dim(gathered, col_start, cols, 0)
    col_normed = (layer_norm(col_nodes.astype(jnp.float32), 1) * node_gain).astype(jnp.bfloat16)
    keyval = jnp.dot(col_normed, w_qkv[:, width:], preferred_element_type=jnp.float32).astype(
        jnp.bfloat16
    )
    col_ints = lax.dynamic_slice_in_dim(all_ints, col_start, cols, 0)
    key = keyval[:, :width].reshape(cols, heads, head_size)
    value_rows = keyval[:, width:].reshape(cols, heads, head_size)
    query_rows = query_rows.reshape(rows, heads, head_size)
    chain_c = col_ints[:, 0]
    res_c = col_ints[:, 1]
    valid_c = col_ints[:, 2] == 1
    block = 16
    count = rows // block

    def one_block(index):
        start = index * block
        zb = lax.dynamic_slice_in_dim(pairs, start, block, 1)
        qb = lax.dynamic_slice_in_dim(query_rows, start, block, 0)
        chain_r = lax.dynamic_slice_in_dim(chain_ids, start, block, 0)
        res_r = lax.dynamic_slice_in_dim(residue_index, start, block, 0)
        return pair_block(
            zb,
            qb,
            key,
            value_rows,
            chain_r,
            res_r,
            chain_c,
            res_c,
            valid_c,
            pair_gain,
            w_bias_gate,
            rel_table,
            w_edge,
            edge_norm_gain,
            w_mlp_in,
            w_mlp_out,
        )

    numer_blocks, denom_blocks, out_blocks = lax.map(one_block, jnp.arange(count, dtype=jnp.int32))
    numer_flat = numer_blocks.reshape(rows, width)
    denom_all = jnp.transpose(denom_blocks, (0, 2, 1)).reshape(rows, heads)
    pairs_out = jnp.transpose(out_blocks, (1, 0, 2, 3)).reshape(chans, rows, cols)
    numer_sum, denom_sum = lax.psum((numer_flat, denom_all), "col")
    attended = (
        (numer_sum.reshape(rows, heads, head_size) / denom_sum[:, :, None])
        .reshape(rows, width)
        .astype(jnp.bfloat16)
    )
    node_update = jnp.dot(attended, w_out, preferred_element_type=jnp.float32).astype(jnp.bfloat16)
    return (node_update, pairs_out)


def solution(mesh):
    in_specs = (
        P(("groups", "row"), None),
        P(("groups", "row")),
        P(("groups", "row")),
        P(("groups", "row")),
        P(None, ("groups", "row"), "col"),
        P(),
        P(),
        P(),
        P(),
        P(),
        P(),
        P(),
        P(),
        P(),
        P(),
    )
    out_specs = (P(("groups", "row"), None), P(None, ("groups", "row"), "col"))
    return jax.shard_map(body, mesh=mesh, in_specs=in_specs, out_specs=out_specs, check_vma=False)
```

profile of v0, /device:TPU:1, one launch (start us, length us, event | category | flops | bytes accessed | tf_op | source)
XLA Modules:
  0.0 160.5 jit_solution(1021016219840302518)
XLA Ops:
  7.2 17.5 %all_gather.7 = bf16[512,768]{1,0:T(8,128)(2,1)S(1)} all-gather(bf16[64,768]{1,0:T(8,128)(2,1)} %param.17), channel_id=1, replica_groups=mesh['groups'=2,'row'=8,'col'=2] {'row'}, dimensions={0}, use_global_device_ids=true | all-gather | bytes 884736 | tf_op jit(solution)/shard_map/all_gather | solution.py:102
  24.7 1.0 convert_reduce_fusion.2
  26.1 2.5 %convolution_convert_fusion = bf16[256,1536]{1,0:T(8,128)(2,1)S(1)} fusion(bf16[768,2304]{1,0:T(8,128)(2,1)} %param.23, f32[768]{0:T(1024)} %param.22, f32[256]{0:T(256)S(1)} %add_rsqrt_fusion.2, f32[256]{0:T(256)S(1)} %broadcast_multiply_fusion.2, bf16[512,768]{1,0:T(8,128)(2,1)S(1)} %all_gather.7, s32[]{:T(128)S(6)} %select_n.25), kind=kOutput, calls=%fused_computation.55 | convolution fusion | flops 605356032 | bytes 3545092 | tf_op jit(solution)/shard_map/dot_general | solution.py:107
  28.7 0.9 fusion.61
  29.7 2.1 %copy.40 = bf16[256,768]{0,1:T(8,128)(2,1)} copy(bf16[256,768]{1,0:T(8,128)(2,1)} %get-tuple-element.249) | data formatting | bytes 786432 | tf_op jit(solution)/shard_map/slice | solution.py:111
  31.7 1.9 %copy.41 = bf16[256,768]{0,1:T(8,128)(2,1)} copy(bf16[256,768]{1,0:T(8,128)(2,1)} %get-tuple-element.248) | data formatting | bytes 786432 | tf_op jit(solution)/shard_map/slice | solution.py:112
  33.7 0.7 add_bitcast_fusion
  34.4 12.7 %all-gather = s32[8,64,3]{1,2,0:T(4,128)S(1)} all-gather(s32[1,64,3]{1,2,0:T(4,128)S(1)} %add_bitcast_fusion), channel_id=1, replica_groups=mesh['groups'=2,'row'=8,'col'=2] {'row'}, dimensions={0}, use_global_device_ids=true | all-gather | bytes 6912 | tf_op jit(solution)/shard_map/all_gather | solution.py:103
  47.7 0.6 compare_reduce_fusion
  48.5 2.3 %fusion.36 = bf16[64,768]{1,0:T(8,128)(2,1)} fusion(bf16[768,2304]{1,0:T(8,128)(2,1)} %param.23, bf16[64,768]{1,0:T(8,128)(2,1)S(1)} %copy-done.4, f32[768]{0:T(1024)S(1)} %copy-done.10, f32[64]{0:T(128)S(1)} %add_rsqrt_fusion.3, f32[64]{0:T(128)S(1)} %broadcast_multiply_fusion.3), kind=kOutput, calls=%fused_computation.59 | convolution fusion | flops 75792384 | bytes 1379840 | tf_op jit(solution)/shard_map/dot_general | solution.py:98
  50.8 1.1 copy.39
  52.5 74.8 %while.14 = (s32[]{:T(128)}, f32[4,16,48,16]{3,2,1,0:T(8,128)}, f32[4,48,16]{2,1,0:T(8,128)}, bf16[4,64,16,256]{3,2,1,0:T(8,128)(2,1)}, pred[256]{0:T(512)(128)(...) while((s32[]{:T(128)}, f32[4,16,48,16]{3,2,1,0:T(8,128)}, ...), condition=%wide.region_10.11_spmd, body=%wide.region_4.10_spmd.sunk | while | flops 530353408 | bytes 40929680 | solution.py:145
  52.5 1.3 dynamic_slice.51
  54.7 0.8 multiply_convert_fusion.7
  56.8 0.7 dynamic_slice.52
  57.6 0.7 dynamic_slice.53
  58.3 0.7 select_bitcast_fusion.2
  59.9 1.4 fusion.101
  62.7 3.6 %fusion.103 = bf16[64,4096]{1,0:T(8,128)(2,1)} fusion(f32[64,4096]{1,0:T(8,128)S(1)} %get-tuple-element.391, bf16[64,256]{1,0:T(8,128)(2,1)} %get-tuple-element.463, bf16[256,64]{0,1:T(8,128)(2,1)} %get-tuple-element.462, f32[64]{0:T(128)} %get-tuple-element.461, f32[4096]{0:T(1024)S(1)} %add_rsqrt_fusion.7, f32[4096]{0:T(1024)S(1)} %broadcast_multiply_fusion.7), kind=kOutput, calls=%fused_computation.7.clone.1 | convolution fusion | flops 279445504 | bytes 1671424 | tf_op jit(solution)/shard_map/while/body/eval_jaxpr/dot_general | solution.py:70
  66.3 1.3 copy.81
  67.6 0.8 bitcast_dynamic-update-slice_fusion.5
  68.4 1.3 convolution_bitcast_fusion.8
  69.7 0.9 copy_dynamic-update-slice_fusion.2
  70.6 0.6 bitcast_dynamic-update-slice_fusion.4
  71.2 1.3 dynamic_slice.51
  73.4 0.8 multiply_convert_fusion.7
  75.5 0.7 dynamic_slice.52
  76.3 0.7 dynamic_slice.53
  77.0 0.7 select_bitcast_fusion.2
  78.6 1.4 fusion.101
  81.3 3.6 %fusion.103 = bf16[64,4096]{1,0:T(8,128)(2,1)} fusion(f32[64,4096]{1,0:T(8,128)S(1)} %get-tuple-element.391, bf16[64,256]{1,0:T(8,128)(2,1)} %get-tuple-element.463, bf16[256,64]{0,1:T(8,128)(2,1)} %get-tuple-element.462, f32[64]{0:T(128)} %get-tuple-element.461, f32[4096]{0:T(1024)S(1)} %add_rsqrt_fusion.7, f32[4096]{0:T(1024)S(1)} %broadcast_multiply_fusion.7), kind=kOutput, calls=%fused_computation.7.clone.1 | convolution fusion | flops 279445504 | bytes 1671424 | tf_op jit(solution)/shard_map/while/body/eval_jaxpr/dot_general | solution.py:70
  84.9 1.3 copy.81
  86.2 0.8 bitcast_dynamic-update-slice_fusion.5
  87.1 1.3 convolution_bitcast_fusion.8
  88.4 0.9 copy_dynamic-update-slice_fusion.2
  89.3 0.6 bitcast_dynamic-update-slice_fusion.4
  89.9 1.3 dynamic_slice.51
  92.1 0.8 multiply_convert_fusion.7
  94.2 0.7 dynamic_slice.52
  95.0 0.7 dynamic_slice.53
  95.7 0.7 select_bitcast_fusion.2
  97.3 1.4 fusion.101
  100.1 3.6 %fusion.103 = bf16[64,4096]{1,0:T(8,128)(2,1)} fusion(f32[64,4096]{1,0:T(8,128)S(1)} %get-tuple-element.391, bf16[64,256]{1,0:T(8,128)(2,1)} %get-tuple-element.463, bf16[256,64]{0,1:T(8,128)(2,1)} %get-tuple-element.462, f32[64]{0:T(128)} %get-tuple-element.461, f32[4096]{0:T(1024)S(1)} %add_rsqrt_fusion.7, f32[4096]{0:T(1024)S(1)} %broadcast_multiply_fusion.7), kind=kOutput, calls=%fused_computation.7.clone.1 | convolution fusion | flops 279445504 | bytes 1671424 | tf_op jit(solution)/shard_map/while/body/eval_jaxpr/dot_general | solution.py:70
  103.7 1.3 copy.81
  105.0 0.9 bitcast_dynamic-update-slice_fusion.5
  105.8 1.3 convolution_bitcast_fusion.8
  107.2 0.9 copy_dynamic-update-slice_fusion.2
  108.6 1.3 dynamic_slice.51
  110.8 0.8 multiply_convert_fusion.7
  113.0 0.7 dynamic_slice.52
  113.7 0.7 dynamic_slice.53
  114.4 0.7 select_bitcast_fusion.2
  116.0 1.4 fusion.101
  118.8 3.6 %fusion.103 = bf16[64,4096]{1,0:T(8,128)(2,1)} fusion(f32[64,4096]{1,0:T(8,128)S(1)} %get-tuple-element.391, bf16[64,256]{1,0:T(8,128)(2,1)} %get-tuple-element.463, bf16[256,64]{0,1:T(8,128)(2,1)} %get-tuple-element.462, f32[64]{0:T(128)} %get-tuple-element.461, f32[4096]{0:T(1024)S(1)} %add_rsqrt_fusion.7, f32[4096]{0:T(1024)S(1)} %broadcast_multiply_fusion.7), kind=kOutput, calls=%fused_computation.7.clone.1 | convolution fusion | flops 279445504 | bytes 1671424 | tf_op jit(solution)/shard_map/while/body/eval_jaxpr/dot_general | solution.py:70
  122.4 1.3 copy.81
  123.7 0.9 bitcast_dynamic-update-slice_fusion.5
  124.5 1.3 convolution_bitcast_fusion.8
  125.9 0.9 copy_dynamic-update-slice_fusion.2
  127.3 2.6 %reshape.151 = f32[64,768]{1,0:T(8,128)} reshape(f32[4,16,48,16]{3,2,1,0:T(8,128)} %get-tuple-element.470) | data formatting | bytes 393216 | tf_op jit(solution)/shard_map/reshape | solution.py:146
  130.0 3.2 %copy.47 = bf16[64,4,16,256]{3,2,1,0:T(8,128)(2,1)} copy(bf16[64,4,16,256]{3,2,0,1:T(8,128)(2,1)} %bitcast.163) | data formatting | bytes 4194304 | tf_op jit(solution)/shard_map/transpose | solution.py:148
  133.2 1.0 copy.44
  134.2 6.5 %psum.15 = f32[64,48]{1,0:T(8,128)S(1)} all-reduce(f32[64,48]{1,0:T(8,128)S(1)} %bitcast.167), channel_id=1, replica_groups=mesh['groups'=2,'row'=8,'col'=2] {'col'}, use_global_device_ids=true, to_apply=%region_12.13 | all-reduce | flops 3072 | bytes 24576 | tf_op jit(solution)/shard_map/psum | solution.py:149
  140.9 10.9 %all-reduce.2.cloned.1.call-done = f32[64,768]{1,0:T(8,128)} async-done(((f32[64,768]{1,0:T(8,128)}), f32[64,768]{1,0:T(8,128)}) %all-reduce.2.cloned.1.call-update) | async-done | bytes 196624 | tf_op jit(solution)/shard_map/psum | solution.py:149
  151.8 1.9 %convolution_convert_fusion.1 = bf16[64,768]{1,0:T(8,128)(2,1)} fusion(bf16[768,768]{1,0:T(8,128)(2,1)S(1)} %copy-done, f32[64,768]{1,0:T(8,128)} %all-reduce.2.cloned.1.call-done, f32[64,768]{1,0:T(8,128)S(1)} %copy.46), kind=kOutput, calls=%fused_computation.60 | convolution fusion | flops 75644928 | bytes 1671168 | tf_op jit(solution)/shard_map/dot_general | solution.py:155
  (137 shorter events, 18.4 us)
Async XLA Ops:
  7.2 144.6 %copy-start = (bf16[768,768]{1,0:T(8,128)(2,1)S(1)}, bf16[768,768]{1,0:T(8,128)(2,1)}, u32[]{:S(2)}) copy-start(bf16[768,768]{1,0:T(8,128)(2,1)} %param.24) | copy-start | bytes 3538948
  7.2 144.6 %all-reduce.2.cloned.1.call-start = ((), (), s32[]{:S(2)}) async-start(), calls=%async_computation | async-start | bytes 393216 | tf_op jit(solution)/shard_map/psum | solution.py:149
  28.7 5.0 %copy-start.9 = (s32[64]{0:T(128)S(1)}, s32[64]{0:T(128)}, u32[]{:S(2)}) copy-start(s32[64]{0:T(128)} %param.20) | copy-start | bytes 772
  28.7 19.6 %copy-start.4 = (bf16[64,768]{1,0:T(8,128)(2,1)S(1)}, bf16[64,768]{1,0:T(8,128)(2,1)}, u32[]{:S(2)}) copy-start(bf16[64,768]{1,0:T(8,128)(2,1)} %param.17) | copy-start | bytes 294916
  28.7 19.8 %copy-start.10 = (f32[768]{0:T(1024)S(1)}, f32[768]{0:T(1024)}, u32[]{:S(2)}) copy-start(f32[768]{0:T(1024)} %param.22) | copy-start | bytes 9220
  29.7 22.8 %copy-start.1 = (bf16[64,64,256]{2,1,0:T(8,128)(2,1)S(1)}, bf16[64,64,256]{2,1,0:T(8,128)(2,1)}, u32[]{:S(2)}) copy-start(bf16[64,64,256]{2,1,0:T(8,128)(2,1)} %param.21) | copy-start | bytes 6291460
  29.7 22.8 %copy-start.5 = (f32[48,66]{1,0:T(8,128)S(1)}, f32[48,66]{1,0:T(8,128)}, u32[]{:S(2)}) copy-start(f32[48,66]{1,0:T(8,128)} %param.27) | copy-start | bytes 38020
  29.7 22.8 %copy-start.6 = (bf16[96,64]{0,1:T(8,128)(2,1)S(1)}, bf16[96,64]{0,1:T(8,128)(2,1)}, u32[]{:S(2)}) copy-start(bf16[96,64]{0,1:T(8,128)(2,1)} %param.26) | copy-start | bytes 36868
  29.7 22.8 %copy-start.7 = (bf16[64,48]{0,1:T(8,128)(2,1)S(1)}, bf16[64,48]{0,1:T(8,128)(2,1)}, u32[]{:S(2)}) copy-start(bf16[64,48]{0,1:T(8,128)(2,1)} %param.28) | copy-start | bytes 18436
  56.6 3.3 %copy-start.3 = (bf16[256,48,16]{0,2,1:T(8,128)(2,1)S(1)}, bf16[256,48,16]{0,2,1:T(8,128)(2,1)}, u32[]{:S(2)}) copy-start(bf16[256,48,16]{0,2,1:T(8,128)(2,1)} %get-tuple-element.450) | copy-start | bytes 1179652 | tf_op jit(solution)/shard_map/while
  56.6 3.3 %copy-start.8 = (pred[256]{0:T(512)(128)(4,1)S(1)}, pred[256]{0:T(512)(128)(4,1)}, u32[]{:S(2)}) copy-start(pred[256]{0:T(512)(128)(4,1)} %get-tuple-element.447) | copy-start | bytes 772 | tf_op jit(solution)/shard_map/while
  66.3 5.0 %copy-start.2 = (bf16[64,64,256]{2,1,0:T(8,128)(2,1)S(1)}, bf16[64,64,256]{2,1,0:T(8,128)(2,1)}, u32[]{:S(2)}) copy-start(bf16[64,64,256]{2,1,0:T(8,128)(2,1)} %get-tuple-element.494) | copy-start | bytes 6291460 | tf_op jit(solution)/shard_map/while
  75.3 3.3 %copy-start.3 = (bf16[256,48,16]{0,2,1:T(8,128)(2,1)S(1)}, bf16[256,48,16]{0,2,1:T(8,128)(2,1)}, u32[]{:S(2)}) copy-start(bf16[256,48,16]{0,2,1:T(8,128)(2,1)} %get-tuple-element.450) | copy-start | bytes 1179652 | tf_op jit(solution)/shard_map/while
  75.3 3.3 %copy-start.8 = (pred[256]{0:T(512)(128)(4,1)S(1)}, pred[256]{0:T(512)(128)(4,1)}, u32[]{:S(2)}) copy-start(pred[256]{0:T(512)(128)(4,1)} %get-tuple-element.447) | copy-start | bytes 772 | tf_op jit(solution)/shard_map/while
  84.9 5.0 %copy-start.2 = (bf16[64,64,256]{2,1,0:T(8,128)(2,1)S(1)}, bf16[64,64,256]{2,1,0:T(8,128)(2,1)}, u32[]{:S(2)}) copy-start(bf16[64,64,256]{2,1,0:T(8,128)(2,1)} %get-tuple-element.494) | copy-start | bytes 6291460 | tf_op jit(solution)/shard_map/while
  94.0 3.3 %copy-start.3 = (bf16[256,48,16]{0,2,1:T(8,128)(2,1)S(1)}, bf16[256,48,16]{0,2,1:T(8,128)(2,1)}, u32[]{:S(2)}) copy-start(bf16[256,48,16]{0,2,1:T(8,128)(2,1)} %get-tuple-element.450) | copy-start | bytes 1179652 | tf_op jit(solution)/shard_map/while
  94.0 3.3 %copy-start.8 = (pred[256]{0:T(512)(128)(4,1)S(1)}, pred[256]{0:T(512)(128)(4,1)}, u32[]{:S(2)}) copy-start(pred[256]{0:T(512)(128)(4,1)} %get-tuple-element.447) | copy-start | bytes 772 | tf_op jit(solution)/shard_map/while
  103.7 5.0 %copy-start.2 = (bf16[64,64,256]{2,1,0:T(8,128)(2,1)S(1)}, bf16[64,64,256]{2,1,0:T(8,128)(2,1)}, u32[]{:S(2)}) copy-start(bf16[64,64,256]{2,1,0:T(8,128)(2,1)} %get-tuple-element.494) | copy-start | bytes 6291460 | tf_op jit(solution)/shard_map/while
  112.7 3.3 %copy-start.3 = (bf16[256,48,16]{0,2,1:T(8,128)(2,1)S(1)}, bf16[256,48,16]{0,2,1:T(8,128)(2,1)}, u32[]{:S(2)}) copy-start(bf16[256,48,16]{0,2,1:T(8,128)(2,1)} %get-tuple-element.450) | copy-start | bytes 1179652 | tf_op jit(solution)/shard_map/while
  112.7 3.3 %copy-start.8 = (pred[256]{0:T(512)(128)(4,1)S(1)}, pred[256]{0:T(512)(128)(4,1)}, u32[]{:S(2)}) copy-start(pred[256]{0:T(512)(128)(4,1)} %get-tuple-element.447) | copy-start | bytes 772 | tf_op jit(solution)/shard_map/while
  122.4 5.0 %copy-start.2 = (bf16[64,64,256]{2,1,0:T(8,128)(2,1)S(1)}, bf16[64,64,256]{2,1,0:T(8,128)(2,1)}, u32[]{:S(2)}) copy-start(bf16[64,64,256]{2,1,0:T(8,128)(2,1)} %get-tuple-element.494) | copy-start | bytes 6291460 | tf_op jit(solution)/shard_map/while
Sparse Core Ops, SparseCore 0:
  130.1 21.6 all-reduce.1
where the time goes:
time: 163 us; the launch traced here: 161 us
  local copies, waits for them, and re-layouts  46.5 us (29%)
  matrix products  37.1 us (23%)
  blocking collectives  36.7 us (23%)
  between operations  14.2 us (9%)
  other arithmetic  12.3 us (8%)
  waiting for transfers between devices  10.9 us (7%)
  loops' own time  2.9 us (2%)
    all_gather x1, blocking collectives, body(): lax.all_gather(nodes, 'row', axis=0, tiled=True)  17.5 us
    dot_general x4, matrix products, pair_block(): out = first + jnp.dot(w_mlp_out, hidden, preferred_element_type=jnp.float32)  14.4 us
    all_gather x1, blocking collectives, body(): lax.all_gather(node_ints, 'row', axis=0, tiled=True)  12.7 us
    while x56, local copies, waits for them, and re-layouts  11.9 us
    psum x1, waiting for transfers between devices, body(): numer_sum, denom_sum = lax.psum((numer_flat, denom_all), 'col')  10.9 us
    dynamic_update_slice x12, local copies, waits for them, and re-layouts, body(): lax.map(one_block, jnp.arange(count, dtype=jnp.int32))  9.32 us
    psum x1, blocking collectives, body(): numer_sum, denom_sum = lax.psum((numer_flat, denom_all), 'col')  6.48 us
    dot_general x4, matrix products, pair_block(): jnp.einsum('axt,zxt->xaz', query_rows, key, preferred_element_type=jnp.fl...  5.5 us
  transfers between devices with their start and end apart: 1, of which 1 were waited for; matrix products, arithmetic and copies ran while one was open for 3% of the time, Pallas kernels for 0%

commit v1 on v0

v1 whole, which is shorter than its diff:
```python
import functools
import jax
import jax.numpy as jnp
from jax import lax
from jax.experimental import pallas as pl
from jax.experimental.pallas import tpu as pltpu
from jax.sharding import PartitionSpec as P

IB = 16
SUB = 8
GELU_A = 2.0 * (2.0 / 3.141592653589793) ** 0.5
GELU_B = GELU_A * 4.0 * 0.044715


def node_norm(values, gain):
    mean = jnp.mean(values, axis=1, keepdims=True)
    var = jnp.mean(jnp.square(values - mean), axis=1, keepdims=True)
    return ((values - mean) * lax.rsqrt(var + 1e-05) * gain).astype(jnp.bfloat16)


def chan_norm(values, gain):
    inv = 1.0 / values.shape[0]
    mean = jnp.sum(values, axis=0, keepdims=True) * inv
    cent = values - mean
    var = jnp.sum(cent * cent, axis=0, keepdims=True) * inv
    return (cent * lax.rsqrt(var + 1e-05) * gain).astype(jnp.bfloat16)


def pair_kernel(
    radius,
    chain_r,
    res_r,
    pairs_ref,
    q_ref,
    kt_ref,
    v_ref,
    cols_ref,
    wcat_ref,
    pgain_ref,
    egain_ref,
    wedge_ref,
    win_ref,
    wout_ref,
    mask_ref,
    numer_ref,
    denom_ref,
    out_ref,
    zs,
    os,
    qb,
    gb,
):
    step = pl.program_id(0)
    chans, iblk, cols = pairs_ref.shape
    heads = wedge_ref.shape[1]
    cpad = (wcat_ref.shape[1] - chans) // 2
    lanes = 128
    nl = cols // lanes
    for t in range(nl):
        zs[t] = (
            pairs_ref[:, :, t * lanes : (t + 1) * lanes]
            .astype(jnp.float32)
            .reshape(chans * iblk, lanes)
        )
    chain_c = cols_ref[0:1, :]
    res_c = cols_ref[1:2, :]
    valid = (cols_ref[2:3, :] == 1).astype(jnp.float32)
    class_ids = lax.broadcasted_iota(jnp.int32, (cpad, cols), 0)

    @pl.when(step == 0)
    def _():
        denom_ref[...] = jnp.zeros_like(denom_ref)

    lane_ids = lax.broadcasted_iota(jnp.int32, denom_ref.shape, 1)

    def sub_block(s, carry):
        base = pl.multiple_of(s * SUB, SUB)
        for u in range(SUB):
            row = q_ref[pl.ds(base + u, 1), :]
            qb[u * heads : (u + 1) * heads, :] = (row * mask_ref[...]).astype(jnp.bfloat16)
        scores = jnp.dot(qb[...], kt_ref[...], preferred_element_type=jnp.float32)
        for u in range(SUB):
            i = base + u
            gi = step * iblk + i
            z = jnp.concatenate([zs[t, pl.ds(i, chans, stride=iblk), :] for t in range(nl)], axis=1)
            pnorm = chan_norm(z, pgain_ref[...])
            offset = jnp.clip(res_r[gi] - res_c, -radius, radius) + radius
            cls = jnp.where(chain_c == chain_r[gi], offset, 2 * radius + 1)
            hot = jnp.where(class_ids == cls, 1.0, 0.0).astype(jnp.bfloat16)
            rhs = jnp.concatenate([pnorm, hot, hot], axis=0)
            bias_gate = jnp.dot(wcat_ref[...], rhs, preferred_element_type=jnp.float32)
            logits = jnp.clip(
                scores[u * heads : (u + 1) * heads] + bias_gate[:heads], -5.0, 5.0
            )
            weights = jnp.exp(logits) * valid
            sig = 0.5 * jnp.tanh(0.5 * bias_gate[heads:]) + 0.5
            gb[u * heads : (u + 1) * heads, :] = (weights * sig).astype(jnp.bfloat16)
            dsum = jnp.sum(weights, axis=1, keepdims=True)
            denom_ref[...] = jnp.where(lane_ids == gi, dsum, denom_ref[...])
            first = z + jnp.dot(
                wedge_ref[...], logits.astype(jnp.bfloat16), preferred_element_type=jnp.float32
            )
            enorm = chan_norm(first, egain_ref[...])
            y = jnp.dot(win_ref[...], enorm, preferred_element_type=jnp.float32)
            arg = y * (GELU_A + GELU_B * (y * y))
            hidden = (y + y * jnp.tanh(arg)).astype(jnp.bfloat16)
            res = first + jnp.dot(wout_ref[...], hidden, preferred_element_type=jnp.float32)
            for t in range(nl):
                os[t, pl.ds(i, chans, stride=iblk), :] = res[:, t * lanes : (t + 1) * lanes]
        full = jnp.dot(gb[...], v_ref[...], preferred_element_type=jnp.float32)
        width = v_ref.shape[1]
        numer_ref[pl.ds(base, SUB), :] = jnp.sum(
            full.reshape(SUB, heads, width) * mask_ref[...][None], axis=1
        )
        return carry

    lax.fori_loop(0, iblk // SUB, sub_block, 0)
    for t in range(nl):
        out_ref[:, :, t * lanes : (t + 1) * lanes] = (
            os[t].reshape(chans, iblk, lanes).astype(jnp.bfloat16)
        )


def body(
    nodes,
    chain_ids,
    residue_index,
    pad_mask,
    pairs,
    node_gain,
    w_qkv,
    w_out,
    pair_gain,
    w_bias_gate,
    rel_table,
    w_edge,
    edge_norm_gain,
    w_mlp_in,
    w_mlp_out,
):
    rows, width = nodes.shape
    chans, _, cols = pairs.shape
    heads, classes = rel_table.shape
    head_size = width // heads
    radius = (classes - 2) // 2
    bf, f32 = jnp.bfloat16, jnp.float32
    col_start = lax.axis_index("col") * cols
    ints = jnp.stack([chain_ids, residue_index, pad_mask], axis=1).astype(bf)
    packed = jnp.concatenate([nodes, jnp.pad(ints, ((0, 0), (0, 125)))], axis=1)
    gathered = lax.all_gather(packed, "row", axis=0, tiled=True)
    own = node_norm(nodes.astype(f32), node_gain)
    query = 0.25 * jnp.dot(own, w_qkv[:, :width], preferred_element_type=f32).astype(bf).astype(f32)
    col_block = lax.dynamic_slice_in_dim(gathered, col_start, cols, 0)
    col_normed = node_norm(col_block[:, :width].astype(f32), node_gain)
    kt = lax.dot_general(
        w_qkv[:, width : 2 * width],
        col_normed,
        (((0,), (1,)), ((), ())),
        preferred_element_type=f32,
    ).astype(bf)
    value = jnp.dot(col_normed, w_qkv[:, 2 * width :], preferred_element_type=f32).astype(bf)
    col_ints = jnp.pad(col_block[:, width : width + 3].astype(jnp.int32).T, ((0, 5), (0, 0)))
    cpad = -(-classes // 16) * 16
    rel_hi = rel_table.astype(bf)
    rel_lo = (rel_table - lax.reduce_precision(rel_table, 8, 7)).astype(bf)
    grow = ((0, heads), (0, cpad - classes))
    wcat = jnp.concatenate([w_bias_gate, jnp.pad(rel_hi, grow), jnp.pad(rel_lo, grow)], axis=1)
    head_of = lax.broadcasted_iota(jnp.int32, (heads, width), 1) // head_size
    mask = (head_of == lax.broadcasted_iota(jnp.int32, (heads, width), 0)).astype(f32)
    dl = -(-rows // 128) * 128

    def fixed(shape):
        return pl.BlockSpec(shape, lambda i, *_: (0,) * len(shape))

    numer, denom, pairs_out = pl.pallas_call(
        functools.partial(pair_kernel, radius),
        grid_spec=pltpu.PrefetchScalarGridSpec(
            num_scalar_prefetch=2,
            grid=(rows // IB,),
            in_specs=[
                pl.BlockSpec((chans, IB, cols), lambda i, *_: (0, i, 0)),
                pl.BlockSpec((IB, width), lambda i, *_: (i, 0)),
                fixed((width, cols)),
                fixed((cols, width)),
                fixed((8, cols)),
                fixed(wcat.shape),
                fixed((chans, 1)),
                fixed((chans, 1)),
                fixed(w_edge.shape),
                fixed(w_mlp_in.shape),
                fixed(w_mlp_out.shape),
                fixed(mask.shape),
            ],
            out_specs=[
                pl.BlockSpec((IB, width), lambda i, *_: (i, 0)),
                fixed((heads, dl)),
                pl.BlockSpec((chans, IB, cols), lambda i, *_: (0, i, 0)),
            ],
            scratch_shapes=[
                pltpu.VMEM((cols // 128, chans * IB, 128), f32),
                pltpu.VMEM((cols // 128, chans * IB, 128), f32),
                pltpu.VMEM((SUB * heads, width), bf),
                pltpu.VMEM((SUB * heads, cols), bf),
            ],
        ),
        out_shape=[
            jax.ShapeDtypeStruct((rows, width), f32),
            jax.ShapeDtypeStruct((heads, dl), f32),
            jax.ShapeDtypeStruct((chans, rows, cols), bf),
        ],
        compiler_params=pltpu.CompilerParams(vmem_limit_bytes=48 << 20),
        name="pair_block",
    )(
        chain_ids,
        residue_index,
        pairs,
        query,
        kt,
        value,
        col_ints,
        wcat,
        pair_gain[:, None],
        edge_norm_gain[:, None],
        w_edge,
        0.5 * w_mlp_in,
        w_mlp_out,
        mask,
    )
    both = jnp.concatenate([numer, denom[:, :rows].T], axis=1)
    both = lax.psum(both, "col")
    attended = (
        (both[:, :width].reshape(rows, heads, head_size) / both[:, width:, None])
        .reshape(rows, width)
        .astype(bf)
    )
    node_update = jnp.dot(attended, w_out, preferred_element_type=f32).astype(bf)
    return (node_update, pairs_out)


def solution(mesh):
    split = P(("groups", "row"))
    in_specs = (
        P(("groups", "row"), None),
        split,
        split,
        split,
        P(None, ("groups", "row"), "col"),
    ) + (P(),) * 10
    out_specs = (P(("groups", "row"), None), P(None, ("groups", "row"), "col"))
    return jax.shard_map(body, mesh=mesh, in_specs=in_specs, out_specs=out_specs, check_vma=False)
```

time: 163 us -> 127 us (0.78)
  Pallas kernels: 0 us -> 37.7 us
  local copies, waits for them, and re-layouts: 46.5 us -> 14.2 us
  matrix products: 37.1 us -> 8.15 us
  blocking collectives: 36.7 us -> 17.5 us
  waiting for transfers between devices: 10.9 us -> 23.4 us
  loops' own time: 2.9 us -> 0 us
  other arithmetic: 12.3 us -> 9.96 us
    pallas_call x0 -> x1, Pallas kernels: none -> 37.7 us  [body(): pl.pallas_call(functools.partial(pair_kernel, radius), grid_spec=pltpu.Pr...]
    dot_general x27 -> x4, matrix products: 37.1 us -> 8.15 us  [the longest x1 2.82 us: body(): lax.dot_general(w_qkv[:, width:2 * width], col_normed, (((0,), (1,)), (()...]
    all_gather x2 -> x1, blocking collectives: 30.2 us -> 17.5 us  [body(): gathered = lax.all_gather(packed, 'row', axis=0, tiled=True)]
    psum x1, waiting for transfers between devices: 10.9 us -> 23.4 us  [body(): both = lax.psum(both, 'col')]
    while x56 -> x0, local copies, waits for them, and re-layouts: 11.9 us -> none
    dynamic_slice x12 -> x0, local copies, waits for them, and re-layouts: 10.9 us -> none  [the longest x4 5.06 us: body(): lax.map(one_block, jnp.arange(count, dtype=jnp.int32))]
    unnamed x17 -> x48, local copies, waits for them, and re-layouts: 0.12 us -> 10.1 us
    dynamic_update_slice x12 -> x0, local copies, waits for them, and re-layouts: 9.32 us -> none  [body(): lax.map(one_block, jnp.arange(count, dtype=jnp.int32))]
  transfers between devices with their start and end apart: 1 -> 1, of which waited for: 1 -> 1; matrix products, arithmetic and copies ran while one was open for 3% -> 0% of each run, Pallas kernels for 0% -> 0%
where the time goes in v1:
time: 127 us; the launch traced here: 125 us
  Pallas kernels  37.7 us (30%)
  waiting for transfers between devices  23.4 us (18%)
  blocking collectives  17.5 us (14%)
  local copies, waits for them, and re-layouts  14.2 us (11%)
  between operations  14.2 us (11%)
  other arithmetic  9.96 us (8%)
  matrix products  8.15 us (6%)
    pallas_call x1, Pallas kernels, body(): pl.pallas_call(functools.partial(pair_kernel, radius), grid_spec=pltpu.Pr...  37.7 us
    psum x1, waiting for transfers between devices, body(): both = lax.psum(both, 'col')  23.4 us
    all_gather x1, blocking collectives, body(): gathered = lax.all_gather(packed, 'row', axis=0, tiled=True)  17.5 us
    unnamed x48, local copies, waits for them, and re-layouts  10.1 us
    dot_general x1, matrix products, body(): lax.dot_general(w_qkv[:, width:2 * width], col_normed, (((0,), (1,)), (()...  2.82 us
    dot_general x1, matrix products, body(): jnp.dot(col_normed, w_qkv[:, 2 * width:], preferred_element_type=f32)  2.63 us
  transfers between devices with their start and end apart: 1, of which 1 were waited for; matrix products, arithmetic and copies ran while one was open for 0% of the time, Pallas kernels for 0%

profile of v1, /device:TPU:1, one launch (start us, length us, event | category | flops | bytes accessed | tf_op | source)
XLA Modules:
  0.0 125.2 jit_solution(8786077529740590749)
XLA Ops:
  7.2 0.0 copy-start
  7.2 0.0 all-reduce.6.cloned.1.call-start
  7.2 0.6 fusion.43
  7.8 0.6 iota_shift-right-logical_fusion
  8.4 0.7 convert_bitcast_fusion.2
  9.1 1.0 convert_reduce_fusion.1
  10.1 0.7 convert_bitcast_fusion
  10.8 0.1 copy.62
  10.9 0.9 fusion.27
  11.8 17.5 %all_gather.3 = bf16[512,896]{1,0:T(8,128)(2,1)S(1)} all-gather(bf16[64,896]{1,0:T(8,128)(2,1)S(1)} %fusion.27), channel_id=1, replica_groups=mesh['groups'=2,'row'=8,'col'=2] {'row'}, dimensions={0}, use_global_device_ids=true | all-gather | bytes 1032192 | tf_op jit(solution)/shard_map/all_gather | solution.py:150
  29.3 0.0 copy-start.10
  29.3 0.9 copy-done.10
  30.3 0.2 copy.60
  30.5 0.1 convert_reduce_fusion
  30.6 0.2 fusion.16
  30.8 0.2 copy-done.20
  30.9 2.6 %convolution_convert_fusion.v_ref = bf16[256,768]{1,0:T(8,128)(2,1)} fusion(bf16[768,2304]{1,0:T(8,128)(2,1)} %param.21, bf16[256,768]{0,1:T(8,128)(2,1)S(1)} %copy.60, f32[768]{0:T(1024)S(1)} %copy-done.20, f32[256]{0:T(256)S(1)} %add_rsqrt_fusion, f32[256]{0:T(256)S(1)} %broadcast_multiply_fusion.1), kind=kOutput, calls=%fused_computation | convolution fusion | flops 303169536 | bytes 1971200 | tf_op jit(solution)/shard_map/dot_general | solution.py:161
  33.6 0.0 copy-start.17
  33.6 0.0 copy-start.18
  33.6 0.0 copy-start.13
  33.6 2.8 %fusion.kt_ref = bf16[768,256]{1,0:T(8,128)(2,1)} fusion(bf16[768,2304]{1,0:T(8,128)(2,1)} %param.21, bf16[256,768]{0,1:T(8,128)(2,1)S(1)} %copy.60, f32[768]{0:T(1024)S(1)} %copy-done.20, f32[256]{0:T(256)S(1)} %add_rsqrt_fusion, f32[256]{0:T(256)S(1)} %broadcast_multiply_fusion.1), kind=kOutput, calls=%fused_computation.2 | convolution fusion | flops 303169536 | bytes 1971200 | tf_op jit(solution)/shard_map/dot_general | solution.py:155
  36.4 0.0 copy-done.11
  36.4 0.2 fusion.22
  36.6 0.5 add_rsqrt_fusion.1
  37.2 0.0 copy-done.16
  37.2 0.1 copy.54.wedge_ref
  37.3 0.0 copy-done.15
  37.3 0.7 copy.49
  38.0 0.0 copy-done.14
  38.0 0.6 fusion.44
  38.6 0.0 copy-done.17
  38.6 0.7 copy.52.pgain_ref
  39.3 0.0 copy-done.19
  39.3 0.0 copy-done.18
  39.3 0.7 copy.53.egain_ref
  40.0 0.0 copy-done.13
  40.0 0.1 copy.50
  40.1 1.7 %fusion.11.q_ref = f32[64,768]{1,0:T(8,128)S(1)} fusion(bf16[768,2304]{1,0:T(8,128)(2,1)} %param.21, bf16[64,768]{1,0:T(8,128)(2,1)} %param.15, f32[768]{0:T(1024)} %param.20, f32[64]{0:T(128)} %add_rsqrt_fusion.1, f32[64]{0:T(128)} %copy-done.19), kind=kOutput, calls=%fused_computation.10 | convolution fusion | flops 75890688 | bytes 1479680 | tf_op jit(solution)/shard_map/dot_general | solution.py:152
  41.9 1.5 %dynamic-slice.1 = bf16[256,3]{1,0:T(8,128)(2,1)} dynamic-slice(bf16[512,896]{1,0:T(8,128)(2,1)} %copy-done.10, s32[]{:T(128)S(6)} %select_n.8, s32[]{:T(128)S(6)} %add.42), dynamic_slice_sizes={256,3} | dynamic-slice | bytes 3076 | tf_op jit(solution)/shard_map/slice | solution.py:162
  43.4 1.5 %copy.61 = bf16[256,3]{0,1:T(4,128)(2,1)} copy(bf16[256,3]{1,0:T(8,128)(2,1)} %dynamic-slice.1) | data formatting | bytes 3072
  44.9 0.7 pad_convert_fusion.cols_ref
  45.6 0.9 fusion.39.wcat_ref
  46.4 0.7 fusion.26.mask_ref
  47.1 0.0 copy-done.1
  47.1 0.0 copy-start.2
  47.1 1.0 copy-done.2
  48.1 1.0 copy-done.3
  49.1 0.8 copy-done.5
  49.9 0.8 copy-done.6
  50.6 0.8 copy-done.7
  51.4 0.7 copy-done.8
  52.1 0.7 copy-done.9
  52.7 37.7 %pair_block.1 = (f32[64,768]{1,0:T(8,128)S(1)}, f32[48,128]{1,0:T(8,128)S(1)}, bf16[64,64,256]{2,1,0:T(8,128)(2,1)}) custom-call(s32[64]{0:T(128)S(1)} %copy-done.9, s32[64]{0:T(128)S(1)} %copy-done.8, bf16[64,64,256]{2,1,0:T(8,128)(2,1)S(1)} %copy-done.1, f32[64,768]{1,0:T(8,128)S(1)} %fusion.11.q_ref, bf16[768,256]{1,0:T(8,128)(2,1)S(1)} %copy-done.3, ...), custom_call_target="tpu_custom_call" | custom-call | tf_op jit(solution)/shard_map/pair_block/pallas_call | solution.py:175
  90.4 0.7 copy-done.4
  91.1 0.1 copy.55
  91.2 1.6 %pad_maximum_fusion = f32[64,816]{1,0:T(8,128)} fusion(f32[64,48]{1,0:T(8,128)S(1)} %copy.55, f32[64,768]{1,0:T(8,128)} %copy-done.4), kind=kLoop, calls=%fused_computation.23 | loop fusion | flops 52224 | bytes 417792 | tf_op jit(solution)/shard_map/concatenate | solution.py:229
  92.8 0.0 all-reduce.6.cloned.1.call-update
  92.9 23.4 %all-reduce.6.cloned.1.call-done = f32[64,816]{1,0:T(8,128)} async-done(((f32[64,816]{1,0:T(8,128)}), f32[64,816]{1,0:T(8,128)}) %all-reduce.6.cloned.1.call-update) | async-done | bytes 208912 | tf_op jit(solution)/shard_map/psum | solution.py:230
  116.2 0.8 slice.33
  117.1 0.1 copy.56
  117.2 0.1 copy.57
  117.3 0.0 copy-done
  117.3 0.0 copy-done.12
  117.3 1.0 convolution_convert_fusion.2
  (23 shorter events, 0.1 us)
Async XLA Ops:
  7.2 110.2 %copy-start = (bf16[768,768]{1,0:T(8,128)(2,1)S(1)}, bf16[768,768]{1,0:T(8,128)(2,1)}, u32[]{:S(2)}) copy-start(bf16[768,768]{1,0:T(8,128)(2,1)} %param.22) | copy-start | bytes 3538948
  7.2 109.0 %all-reduce.6.cloned.1.call-start = ((), (), s32[]{:S(2)}) async-start(), calls=%async_computation | async-start | bytes 458752 | tf_op jit(solution)/shard_map/psum | solution.py:230
  29.3 0.9 copy-start.10
  30.2 0.7 copy-start.20
  33.6 2.9 %copy-start.11 = (bf16[64,768]{1,0:T(8,128)(2,1)S(1)}, bf16[64,768]{1,0:T(8,128)(2,1)}, u32[]{:S(2)}) copy-start(bf16[64,768]{1,0:T(8,128)(2,1)} %param.15) | copy-start | bytes 294916
  33.6 3.6 %copy-start.16 = (bf16[64,48]{0,1:T(8,128)(2,1)S(1)}, bf16[64,48]{0,1:T(8,128)(2,1)}, u32[]{:S(2)}) copy-start(bf16[64,48]{0,1:T(8,128)(2,1)} %param.26) | copy-start | bytes 18436
  33.6 3.7 %copy-start.15 = (bf16[96,64]{0,1:T(8,128)(2,1)S(1)}, bf16[96,64]{0,1:T(8,128)(2,1)}, u32[]{:S(2)}) copy-start(bf16[96,64]{0,1:T(8,128)(2,1)} %param.24) | copy-start | bytes 36868
  33.6 4.4 %copy-start.14 = (f32[48,66]{1,0:T(8,128)S(1)}, f32[48,66]{1,0:T(8,128)}, u32[]{:S(2)}) copy-start(f32[48,66]{1,0:T(8,128)} %param.25) | copy-start | bytes 38020
  33.6 5.0 %copy-start.17 = (f32[64]{0:T(128)S(1)}, f32[64]{0:T(128)}, u32[]{:S(2)}) copy-start(f32[64]{0:T(128)} %param.23) | copy-start | bytes 772
  33.6 5.7 %copy-start.18 = (f32[64]{0:T(128)S(1)}, f32[64]{0:T(128)}, u32[]{:S(2)}) copy-start(f32[64]{0:T(128)} %param.27) | copy-start | bytes 772
  33.6 6.4 %copy-start.13 = (bf16[256,64]{0,1:T(8,128)(2,1)S(1)}, bf16[256,64]{0,1:T(8,128)(2,1)}, u32[]{:S(2)}) copy-start(bf16[256,64]{0,1:T(8,128)(2,1)} %param.28) | copy-start | bytes 98308
  36.4 2.9 %copy-start.19 = (f32[64]{0:T(128)}, f32[64]{0:T(128)S(1)}, u32[]{:S(2)}) copy-start(f32[64]{0:T(128)S(1)} %broadcast_multiply_fusion.2) | copy-start | bytes 772
  39.3 7.8 %copy-start.1 = (bf16[64,64,256]{2,1,0:T(8,128)(2,1)S(1)}, bf16[64,64,256]{2,1,0:T(8,128)(2,1)}, u32[]{:S(2)}) copy-start(bf16[64,64,256]{2,1,0:T(8,128)(2,1)} %pairs_ref.1) | copy-start | bytes 6291460
  47.1 1.0 copy-start.2
  48.1 1.0 copy-start.3
  49.1 0.8 copy-start.5
  49.9 0.8 copy-start.6
  50.6 0.8 copy-start.7
  51.4 0.7 copy-start.8
  52.1 0.7 copy-start.9
  90.4 0.7 copy-start.4
  116.2 1.1 copy-start.12
Sparse Core Ops, SparseCore 0:
  93.0 23.1 all-reduce.5

commit v2 on v1

v2 whole, which is shorter than its diff:
```python
import functools
import jax
import jax.numpy as jnp
from jax import lax
from jax.experimental import pallas as pl
from jax.experimental.pallas import tpu as pltpu
from jax.sharding import PartitionSpec as P

IB = 16
NA = 4
NC = 8
ND = 4
GELU_A = 2.0 * (2.0 / 3.141592653589793) ** 0.5
GELU_B = GELU_A * 4.0 * 0.044715
MESH = pl.DeviceIdType.MESH
BF, F32 = jnp.bfloat16, jnp.float32
LANES = 128


def node_norm(values, gain):
    mean = jnp.mean(values, axis=1, keepdims=True)
    cent = values - mean
    var = jnp.mean(cent * cent, axis=1, keepdims=True)
    return (cent * lax.rsqrt(var + 1e-05) * gain).astype(BF)


def chan_norm(values, gain):
    inv = 1.0 / values.shape[0]
    mean = jnp.sum(values, axis=0, keepdims=True) * inv
    cent = values - mean
    var = jnp.sum(cent * cent, axis=0, keepdims=True) * inv
    return (cent * lax.rsqrt(var + 1e-05) * gain).astype(BF)


def column(row):
    n = row.shape[1]
    eye = lax.broadcasted_iota(jnp.int32, (n, n), 0) == lax.broadcasted_iota(jnp.int32, (n, n), 1)
    return jnp.sum(jnp.where(eye, row, 0.0), axis=1, keepdims=True)


def fused_kernel(
    nrow,
    ncol,
    chain_s,
    res_s,
    ints_ref,
    nodes_ref,
    pairs_hbm,
    wqkv_hbm,
    wo_hbm,
    ngain_ref,
    pgain_ref,
    egain_ref,
    wbg_ref,
    rel_ref,
    wedge_ref,
    win_ref,
    wout_ref,
    node_out,
    pairs_out,
    snd,
    rbuf,
    wqkv,
    wo,
    pin,
    pout,
    zs,
    os,
    bias_s,
    sig_s,
    lg_s,
    qf,
    key,
    val,
    qb,
    nd,
    xbuf,
    pin_sem,
    pout_sem,
    w_sem,
    dsend,
    fsend,
    recv,
    xsend,
    xrecv,
):
    rows, width = nodes_ref.shape
    chans = wbg_ref.shape[1]
    heads, classes = rel_ref.shape
    cols = key.shape[0]
    hsize = width // heads
    radius = (classes - 2) // 2
    npc = cols // rows
    nblk = rows // IB
    nl = cols // LANES
    half = nrow // 2
    r = lax.axis_index("row")
    c = lax.axis_index("col")
    par = lax.rem(r, 2)
    sib = r + 1 - 2 * par
    chip = r // 2
    slot = lax.rem(r, npc)
    is_src = r // npc == c

    def pair_in(b):
        return pltpu.make_async_copy(
            pairs_hbm.at[:, pl.ds(b * IB, IB), :], pin.at[b], pin_sem.at[b]
        )

    def pair_outc(b):
        return pltpu.make_async_copy(
            pout.at[b], pairs_out.at[:, pl.ds(b * IB, IB), :], pout_sem.at[b]
        )

    wq_copy = pltpu.make_async_copy(wqkv_hbm, wqkv, w_sem.at[0])
    wo_copy = pltpu.make_async_copy(wo_hbm, wo, w_sem.at[1])
    for b in range(nblk):
        pair_in(b).start()
    wq_copy.start()
    wo_copy.start()

    barrier = pltpu.get_barrier_semaphore()
    for p in range(1, half):
        peer = lax.rem(chip + p, half) * 2 + par
        pl.semaphore_signal(barrier, inc=1, device_id={"row": peer}, device_id_type=MESH)
    pl.semaphore_signal(barrier, inc=1, device_id={"row": sib}, device_id_type=MESH)
    for p in range(1, ncol):
        pl.semaphore_signal(
            barrier, inc=1, device_id={"col": lax.rem(c + p, ncol)}, device_id_type=MESH
        )
    snd[:, :width] = nodes_ref[...]
    lane = lax.broadcasted_iota(jnp.int32, (rows, LANES), 1)
    tail = jnp.zeros((rows, LANES), F32)
    for k in range(3):
        tail = jnp.where(lane == k, column(ints_ref[k : k + 1, :].astype(F32)), tail)
    snd[:, width:] = tail.astype(BF)
    pl.semaphore_wait(barrier, half + ncol - 1)

    def direct(p):
        peer = lax.rem(chip + p, half) * 2 + par
        return pltpu.make_async_remote_copy(
            src_ref=snd,
            dst_ref=rbuf.at[slot],
            send_sem=dsend.at[p],
            recv_sem=recv.at[slot],
            device_id={"row": peer},
            device_id_type=MESH,
        )

    def forward(k):
        s = 2 * k + par
        return pltpu.make_async_remote_copy(
            src_ref=rbuf.at[s],
            dst_ref=rbuf.at[s],
            send_sem=fsend.at[k],
            recv_sem=recv.at[s],
            device_id={"row": sib},
            device_id_type=MESH,
        )

    def arrived(s):
        return pltpu.make_async_remote_copy(
            src_ref=rbuf.at[s],
            dst_ref=rbuf.at[s],
            send_sem=fsend.at[0],
            recv_sem=recv.at[s],
            device_id={"row": sib},
            device_id_type=MESH,
        )

    @pl.when(is_src)
    def _():
        for p in range(1, half):
            direct(p).start()
        rbuf[slot] = snd[...]

    mask = jnp.where(
        lax.broadcasted_iota(jnp.int32, (heads, width), 1) // hsize
        == lax.broadcasted_iota(jnp.int32, (heads, width), 0),
        1.0,
        0.0,
    )
    pgain = column(pgain_ref[...])
    egain = column(egain_ref[...])
    cpad = -(-classes // 16) * 16
    rel = jnp.concatenate([rel_ref[...], jnp.zeros((heads, cpad - classes), F32)], axis=1)
    rel_hi = rel.astype(BF)
    rel_lo = (rel - rel_hi.astype(F32)).astype(BF)
    rel_cat = jnp.concatenate([rel_hi.astype(F32), rel_lo.astype(F32)], axis=1).astype(BF)

    def wide_rows(b, base, n):
        return jnp.concatenate(
            [
                zs[b, t, pl.ds(base + u, chans, stride=IB), :]
                for u in range(n)
                for t in range(nl)
            ],
            axis=1,
        )

    def spread(b):
        pair_in(b).wait()
        for t in range(nl):
            zs[b, t] = (
                pin[b, :, :, t * LANES : (t + 1) * LANES].astype(F32).reshape(chans * IB, LANES)
            )

    def bias_block(b):
        spread(b)

        def chunk(k, carry):
            base = k * NA
            pnorm = chan_norm(wide_rows(b, base, NA), pgain)
            bg = jnp.dot(wbg_ref[...], pnorm, preferred_element_type=F32)
            sg = 0.5 * jnp.tanh(0.5 * bg[heads:]) + 0.5
            for u in range(NA):
                at = pl.ds(pl.multiple_of((b * IB + base + u) * heads, heads), heads)
                bias_s[at, :] = bg[:heads, u * cols : (u + 1) * cols]
                sig_s[at, :] = sg[:, u * cols : (u + 1) * cols]
            return carry

        lax.fori_loop(0, IB // NA, chunk, 0)

    for b in range(nblk - 1):
        bias_block(b)
    for k in range(npc // 2):
        mine = c * npc + 2 * k + par == r

        @pl.when(jnp.logical_not(mine))
        def _():
            arrived(2 * k + par).wait_recv()

        forward(k).start()
    bias_block(nblk - 1)

    wq_copy.wait()
    own = node_norm(nodes_ref[...].astype(F32), ngain_ref[...])
    query = jnp.dot(own, wqkv[:, :width], preferred_element_type=F32)
    qf[...] = 0.25 * query.astype(BF).astype(F32)
    for k in range(npc // 2):
        arrived(2 * k + 1 - par).wait_recv()
    for s in range(npc):
        normed = node_norm(rbuf[s, :, :width].astype(F32), ngain_ref[...])
        kv = jnp.dot(normed, wqkv[:, width:], preferred_element_type=F32).astype(BF)
        key[s * rows : (s + 1) * rows, :] = kv[:, :width]
        val[s * rows : (s + 1) * rows, :] = kv[:, width:]
    tails = jnp.concatenate([rbuf[s, :, width:] for s in range(npc)], axis=0)
    pick = jnp.where(
        lax.broadcasted_iota(jnp.int32, (8, LANES), 0)
        == lax.broadcasted_iota(jnp.int32, (8, LANES), 1),
        1.0,
        0.0,
    ).astype(BF)
    col_ints = lax.dot_general(
        pick, tails, (((1,), (1,)), ((), ())), preferred_element_type=F32
    )
    chain_c = col_ints[0:1].astype(jnp.int32)
    res_c = col_ints[1:2].astype(jnp.int32)
    valid = jnp.where(col_ints[2:3] == 1.0, 1.0, 0.0)
    class_ids = lax.broadcasted_iota(jnp.int32, (cpad, cols), 0)

    def attend(k, carry):
        base = pl.multiple_of(k * NC, NC)
        at = pl.ds(pl.multiple_of(base * heads, NC * heads), NC * heads)
        rels = []
        for u in range(NC):
            qb[u * heads : (u + 1) * heads, :] = (qf[pl.ds(base + u, 1), :] * mask).astype(BF)
            gi = base + u
            offset = jnp.clip(res_s[gi] - res_c, -radius, radius) + radius
            cls = jnp.where(chain_c == chain_s[gi], offset, 2 * radius + 1)
            hot = jnp.where(class_ids == cls, 1.0, 0.0).astype(BF)
            rels.append(
                jnp.dot(
                    rel_cat, jnp.concatenate([hot, hot], axis=0), preferred_element_type=F32
                )
            )
        scores = lax.dot_general(
            qb[...], key[...], (((1,), (1,)), ((), ())), preferred_element_type=F32
        )
        logits = jnp.clip(scores + bias_s[at, :] + jnp.concatenate(rels, axis=0), -5.0, 5.0)
        lg_s[at, :] = logits.astype(BF)
        weights = jnp.exp(logits) * valid
        gated = (weights * sig_s[at, :]).astype(BF)
        full = jnp.dot(gated, val[...], preferred_element_type=F32)
        dsum = jnp.sum(weights, axis=1, keepdims=True)
        nd[pl.ds(base, NC), :width] = jnp.sum(full.reshape(NC, heads, width) * mask[None], axis=1)
        nd[pl.ds(base, NC), width:] = jnp.sum(dsum.reshape(NC, heads, 1) * mask[None], axis=1)
        return carry

    lax.fori_loop(0, rows // NC, attend, 0)

    def exchange(p):
        return pltpu.make_async_remote_copy(
            src_ref=nd,
            dst_ref=xbuf.at[p - 1],
            send_sem=xsend.at[p - 1],
            recv_sem=xrecv.at[p - 1],
            device_id={"col": lax.rem(c + p, ncol)},
            device_id_type=MESH,
        )

    for p in range(1, ncol):
        exchange(p).start()

    win = (0.5 * win_ref[...].astype(F32)).astype(BF)

    def mlp_block(b, carry):
        def chunk(k, carry):
            base = k * ND
            z = wide_rows(b, base, ND)
            lg = jnp.concatenate(
                [
                    lg_s[
                        pl.ds(pl.multiple_of((b * IB + base + u) * heads, heads), heads), :
                    ]
                    for u in range(ND)
                ],
                axis=1,
            )
            first = z + jnp.dot(wedge_ref[...], lg, preferred_element_type=F32)
            enorm = chan_norm(first, egain)
            y = jnp.dot(win, enorm, preferred_element_type=F32)
            arg = y * (GELU_A + GELU_B * (y * y))
            hidden = (y + y * jnp.tanh(arg)).astype(BF)
            res = first + jnp.dot(wout_ref[...], hidden, preferred_element_type=F32)
            for u in range(ND):
                for t in range(nl):
                    at = u * cols + t * LANES
                    os[t, pl.ds(base + u, chans, stride=IB), :] = res[:, at : at + LANES]
            return carry

        lax.fori_loop(0, IB // ND, chunk, 0)
        for t in range(nl):
            pout[b, :, :, t * LANES : (t + 1) * LANES] = (
                os[t].reshape(chans, IB, LANES).astype(BF)
            )
        pair_outc(b).start()
        return carry

    lax.fori_loop(0, nblk, mlp_block, 0)

    total = nd[...]
    for p in range(1, ncol):
        exchange(p).wait_recv()
        total = total + xbuf[p - 1]
    attended = (total[:, :width] / total[:, width:]).astype(BF)
    wo_copy.wait()
    node_out[...] = jnp.dot(attended, wo[...], preferred_element_type=F32).astype(BF)

    for p in range(1, ncol):
        exchange(p).wait_send()

    @pl.when(is_src)
    def _():
        for p in range(1, half):
            direct(p).wait_send()

    for k in range(npc // 2):
        forward(k).wait_send()
    for b in range(nblk):
        pair_outc(b).wait()


def body(
    nrow,
    ncol,
    nodes,
    chain_ids,
    residue_index,
    pad_mask,
    pairs,
    node_gain,
    w_qkv,
    w_out,
    pair_gain,
    w_bias_gate,
    rel_table,
    w_edge,
    edge_norm_gain,
    w_mlp_in,
    w_mlp_out,
):
    rows, width = nodes.shape
    chans, _, cols = pairs.shape
    heads = rel_table.shape[0]
    npc = cols // rows
    nblk = rows // IB
    nl = cols // LANES
    ints = jnp.stack([chain_ids, residue_index, pad_mask], axis=0)
    vm = pl.BlockSpec(memory_space=pltpu.VMEM)
    sm = pl.BlockSpec(memory_space=pltpu.SMEM)
    hb = pl.BlockSpec(memory_space=pl.ANY)
    dma = pltpu.SemaphoreType.DMA
    return pl.pallas_call(
        functools.partial(fused_kernel, nrow, ncol),
        in_specs=[sm, sm, vm, vm, hb, hb, hb] + [vm] * 8,
        out_specs=[vm, hb],
        out_shape=[
            jax.ShapeDtypeStruct((rows, width), BF),
            jax.ShapeDtypeStruct((chans, rows, cols), BF),
        ],
        scratch_shapes=[
            pltpu.VMEM((rows, width + LANES), BF),
            pltpu.VMEM((npc, rows, width + LANES), BF),
            pltpu.VMEM(w_qkv.shape, BF),
            pltpu.VMEM(w_out.shape, BF),
            pltpu.VMEM((nblk, chans, IB, cols), BF),
            pltpu.VMEM((nblk, chans, IB, cols), BF),
            pltpu.VMEM((nblk, nl, chans * IB, LANES), F32),
            pltpu.VMEM((nl, chans * IB, LANES), F32),
            pltpu.VMEM((rows * heads, cols), F32),
            pltpu.VMEM((rows * heads, cols), F32),
            pltpu.VMEM((rows * heads, cols), BF),
            pltpu.VMEM((rows, width), F32),
            pltpu.VMEM((cols, width), BF),
            pltpu.VMEM((cols, width), BF),
            pltpu.VMEM((NC * heads, width), BF),
            pltpu.VMEM((rows, 2 * width), F32),
            pltpu.VMEM((ncol - 1, rows, 2 * width), F32),
            dma((nblk,)),
            dma((nblk,)),
            dma((2,)),
            dma((nrow // 2,)),
            dma((npc // 2,)),
            dma((npc,)),
            dma((ncol - 1,)),
            dma((ncol - 1,)),
        ],
        compiler_params=pltpu.CompilerParams(
            vmem_limit_bytes=60 << 20, collective_id=0, has_side_effects=True
        ),
        name="fused_layer",
    )(
        chain_ids,
        residue_index,
        ints,
        nodes,
        pairs,
        w_qkv,
        w_out,
        node_gain[None],
        pair_gain[None],
        edge_norm_gain[None],
        w_bias_gate,
        rel_table,
        w_edge,
        w_mlp_in,
        w_mlp_out,
    )


def solution(mesh):
    split = P(("groups", "row"))
    in_specs = (
        P(("groups", "row"), None),
        split,
        split,
        split,
        P(None, ("groups", "row"), "col"),
    ) + (P(),) * 10
    out_specs = (P(("groups", "row"), None), P(None, ("groups", "row"), "col"))
    return jax.shard_map(
        functools.partial(body, mesh.shape["row"], mesh.shape["col"]),
        mesh=mesh,
        in_specs=in_specs,
        out_specs=out_specs,
        check_vma=False,
    )
```

time: 127 us -> 52.9 us (0.42)
  the two profiles are of different devices: /device:TPU:1 before, /device:TPU:14 now
where the time goes in v2:
time: 52.9 us; the launch traced here: 52.5 us
  Pallas kernels  40.3 us (76%)
  local copies, waits for them, and re-layouts  10.3 us (19%)
  other arithmetic  1.28 us (2%)
  between operations  0.64 us (1%)
    pallas_call x1, Pallas kernels, body(): pl.pallas_call(functools.partial(fused_kernel, nrow, ncol), in_specs=[sm,...  40.3 us
    unnamed x5, local copies, waits for them, and re-layouts  8.99 us
    broadcast_in_dim x1, local copies, waits for them, and re-layouts, body(): node_gain[None]  1.28 us
    another operation x1, other arithmetic, body(): ints = jnp.stack([chain_ids, residue_index, pad_mask], axis=0)  1.28 us

profile of v2, /device:TPU:14, one launch (start us, length us, event | category | flops | bytes accessed | tf_op | source)
XLA Modules:
  0.0 52.5 jit_solution(12804485795731060841)
XLA Ops:
  0.6 1.3 %pad_add_fusion.ints_ref = s32[3,64]{1,0:T(4,128)} fusion(s32[1,64]{1,0:T(1,128)} %bitcast.9, s32[1,64]{1,0:T(1,128)} %bitcast.6, s32[1,64]{1,0:T(1,128)} %bitcast.5), kind=kLoop, calls=%fused_computation | loop fusion | flops 384 | bytes 1536 | tf_op jit(solution)/shard_map/stack | solution.py:389
  1.9 1.3 %broadcast_in_dim.9.ngain_ref = f32[1,768]{1,0:T(1,128)} reshape(f32[768]{0:T(1024)} %param.20) | data formatting | bytes 6144 | tf_op jit(solution)/shard_map/broadcast_in_dim | solution.py:441
  3.2 1.4 %copy.18.wedge_ref = bf16[64,48]{1,0:T(8,128)(2,1)} copy(bf16[64,48]{0,1:T(8,128)(2,1)} %param.26) | data formatting | bytes 12288 | tf_op args[11]
  4.6 1.4 %copy.17.wbg_ref = bf16[96,64]{1,0:T(8,128)(2,1)} copy(bf16[96,64]{0,1:T(8,128)(2,1)} %param.24) | data formatting | bytes 24576 | tf_op args[9]
  6.0 1.5 %copy.19.win_ref = bf16[256,64]{1,0:T(8,128)(2,1)} copy(bf16[256,64]{0,1:T(8,128)(2,1)} %param.28) | data formatting | bytes 65536 | tf_op args[13]
  7.5 40.3 %fused_layer.1 = (bf16[64,768]{1,0:T(8,128)(2,1)}, bf16[64,64,256]{2,1,0:T(8,128)(2,1)}) custom-call(s32[64]{0:T(128)} %chain_s.1, s32[64]{0:T(128)} %res_s.1, s32[3,64]{1,0:T(4,128)} %pad_add_fusion.ints_ref, bf16[64,768]{1,0:T(8,128)(2,1)} %nodes_ref.1, bf16[64,64,256]{2,1,0:T(8,128)(2,1)} %pairs_hbm.1, bf16[768,2304]{1,0:T(8,128)(2,1)} %wqkv_hbm.1, ...), custom_call_target="tpu_custom_call" | custom-call | tf_op jit(solution)/shard_map/fused_layer/pallas_call | solution.py:394
  47.8 1.5 %copy.22 = bf16[64,768]{1,0:T(8,128)(2,1)} copy(bf16[64,768]{1,0:T(8,128)(2,1)} %get-tuple-element.4) | data formatting | bytes 196608
  49.3 3.2 %copy.23 = bf16[64,64,256]{2,1,0:T(8,128)(2,1)} copy(bf16[64,64,256]{2,1,0:T(8,128)(2,1)} %get-tuple-element.5) | data formatting | bytes 4194304

commit v3 on v2

--- a/solution.py
+++ b/solution.py
@@ -38,12 +38,26 @@
     return jnp.sum(jnp.where(eye, row, 0.0), axis=1, keepdims=True)
 
 
+def flip(mat):
+    n = mat.shape[0]
+    eye = jnp.where(
+        lax.broadcasted_iota(jnp.int32, (n, n), 0) == lax.broadcasted_iota(jnp.int32, (n, n), 1),
+        1.0,
+        0.0,
+    ).astype(BF)
+    return lax.dot_general(
+        mat, eye, (((0,), (0,)), ((), ())), preferred_element_type=F32
+    ).astype(BF)
+
+
 def fused_kernel(
     nrow,
     ncol,
     chain_s,
     res_s,
-    ints_ref,
+    chain_ref,
+    res_ref,
+    pad_ref,
     nodes_ref,
     pairs_hbm,
     wqkv_hbm,
@@ -59,7 +73,10 @@
     node_out,
     pairs_out,
     snd,
-    rbuf,
+    gbuf,
+    hbuf,
+    sbuf,
+    nbuf,
     wqkv,
     wo,
     pin,
@@ -79,13 +96,15 @@
     pout_sem,
     w_sem,
     dsend,
-    fsend,
-    recv,
+    drecv,
+    hsend,
+    hrecv,
+    ssem,
     xsend,
     xrecv,
 ):
     rows, width = nodes_ref.shape
-    chans = wbg_ref.shape[1]
+    chans = wbg_ref.shape[0]
     heads, classes = rel_ref.shape
     cols = key.shape[0]
     hsize = width // heads
@@ -99,8 +118,8 @@
     par = lax.rem(r, 2)
     sib = r + 1 - 2 * par
     chip = r // 2
-    slot = lax.rem(r, npc)
-    is_src = r // npc == c
+    h2 = npc // 2
+    prow = rows // ncol
 
     def pair_in(b):
         return pltpu.make_async_copy(
@@ -131,48 +150,67 @@
     snd[:, :width] = nodes_ref[...]
     lane = lax.broadcasted_iota(jnp.int32, (rows, LANES), 1)
     tail = jnp.zeros((rows, LANES), F32)
-    for k in range(3):
-        tail = jnp.where(lane == k, column(ints_ref[k : k + 1, :].astype(F32)), tail)
+    for k, ref in enumerate((chain_ref, res_ref, pad_ref)):
+        tail = jnp.where(lane == k, column(ref[...].astype(F32)), tail)
     snd[:, width:] = tail.astype(BF)
     pl.semaphore_wait(barrier, half + ncol - 1)
 
     def direct(p):
         peer = lax.rem(chip + p, half) * 2 + par
         return pltpu.make_async_remote_copy(
-            src_ref=snd,
-            dst_ref=rbuf.at[slot],
+            src_ref=gbuf.at[chip],
+            dst_ref=gbuf.at[chip],
             send_sem=dsend.at[p],
-            recv_sem=recv.at[slot],
+            recv_sem=drecv.at[chip],
             device_id={"row": peer},
             device_id_type=MESH,
         )
 
-    def forward(k):
-        s = 2 * k + par
+    def direct_in(p):
+        j = lax.rem(chip + p, half)
         return pltpu.make_async_remote_copy(
-            src_ref=rbuf.at[s],
-            dst_ref=rbuf.at[s],
-            send_sem=fsend.at[k],
-            recv_sem=recv.at[s],
-            device_id={"row": sib},
+            src_ref=gbuf.at[j],
+            dst_ref=gbuf.at[j],
+            send_sem=dsend.at[p],
+            recv_sem=drecv.at[j],
+            device_id={"row": j * 2 + par},
             device_id_type=MESH,
         )
 
-    def arrived(s):
+    def across(p):
+        c2 = lax.rem(c + p, ncol)
         return pltpu.make_async_remote_copy(
-            src_ref=rbuf.at[s],
-            dst_ref=rbuf.at[s],
-            send_sem=fsend.at[0],
-            recv_sem=recv.at[s],
-            device_id={"row": sib},
+            src_ref=gbuf.at[pl.ds(c2 * h2, h2)],
+            dst_ref=hbuf.at[c],
+            send_sem=hsend.at[p],
+            recv_sem=hrecv.at[c],
+            device_id={"col": c2},
             device_id_type=MESH,
         )
 
-    @pl.when(is_src)
-    def _():
-        for p in range(1, half):
-            direct(p).start()
-        rbuf[slot] = snd[...]
+    def across_in(p):
+        c2 = lax.rem(c + p, ncol)
+        return pltpu.make_async_remote_copy(
+            src_ref=gbuf.at[pl.ds(c2 * h2, h2)],
+            dst_ref=hbuf.at[c2],
+            send_sem=hsend.at[p],
+            recv_sem=hrecv.at[c2],
+            device_id={"col": c2},
+            device_id_type=MESH,
+        )
+
+    twin = pltpu.make_async_remote_copy(
+        src_ref=hbuf,
+        dst_ref=sbuf,
+        send_sem=ssem.at[0],
+        recv_sem=ssem.at[1],
+        device_id={"row": sib},
+        device_id_type=MESH,
+    )
+
+    gbuf[chip] = snd[pl.ds(pl.multiple_of(c * prow, prow), prow), :]
+    for p in range(1, half):
+        direct(p).start()
 
     mask = jnp.where(
         lax.broadcasted_iota(jnp.int32, (heads, width), 1) // hsize
@@ -180,6 +218,10 @@
         1.0,
         0.0,
     )
+    ngain = jnp.concatenate([ngain_ref[k : k + 1, :] for k in range(width // LANES)], axis=1)
+    wbg = flip(wbg_ref[...])
+    wedge = flip(wedge_ref[...])
+    win = (0.5 * flip(win_ref[...]).astype(F32)).astype(BF)
     pgain = column(pgain_ref[...])
     egain = column(egain_ref[...])
     cpad = -(-classes // 16) * 16
@@ -211,7 +253,7 @@
         def chunk(k, carry):
             base = k * NA
             pnorm = chan_norm(wide_rows(b, base, NA), pgain)
-            bg = jnp.dot(wbg_ref[...], pnorm, preferred_element_type=F32)
+            bg = jnp.dot(wbg, pnorm, preferred_element_type=F32)
             sg = 0.5 * jnp.tanh(0.5 * bg[heads:]) + 0.5
             for u in range(NA):
                 at = pl.ds(pl.multiple_of((b * IB + base + u) * heads, heads), heads)
@@ -223,28 +265,32 @@
 
     for b in range(nblk - 1):
         bias_block(b)
-    for k in range(npc // 2):
-        mine = c * npc + 2 * k + par == r
-
-        @pl.when(jnp.logical_not(mine))
-        def _():
-            arrived(2 * k + par).wait_recv()
-
-        forward(k).start()
+    for p in range(1, half):
+        direct_in(p).wait_recv()
+    for p in range(1, ncol):
+        across(p).start()
+    hbuf[c] = gbuf[pl.ds(c * h2, h2)]
     bias_block(nblk - 1)
-
+    for p in range(1, ncol):
+        across_in(p).wait_recv()
+    twin.start()
     wq_copy.wait()
-    own = node_norm(nodes_ref[...].astype(F32), ngain_ref[...])
+    own = node_norm(nodes_ref[...].astype(F32), ngain)
     query = jnp.dot(own, wqkv[:, :width], preferred_element_type=F32)
     qf[...] = 0.25 * query.astype(BF).astype(F32)
-    for k in range(npc // 2):
-        arrived(2 * k + 1 - par).wait_recv()
-    for s in range(npc):
-        normed = node_norm(rbuf[s, :, :width].astype(F32), ngain_ref[...])
-        kv = jnp.dot(normed, wqkv[:, width:], preferred_element_type=F32).astype(BF)
-        key[s * rows : (s + 1) * rows, :] = kv[:, :width]
-        val[s * rows : (s + 1) * rows, :] = kv[:, width:]
-    tails = jnp.concatenate([rbuf[s, :, width:] for s in range(npc)], axis=0)
+    twin.wait_recv()
+    for k in range(h2):
+        for q in range(ncol):
+            at = (2 * k + par) * rows + q * prow
+            nbuf[pl.ds(pl.multiple_of(at, prow), prow), :] = hbuf[q, k]
+            at = (2 * k + 1 - par) * rows + q * prow
+            nbuf[pl.ds(pl.multiple_of(at, prow), prow), :] = sbuf[q, k]
+    normed = node_norm(nbuf[:, :width].astype(F32), ngain)
+    key[...] = jnp.dot(
+        normed, wqkv[:, width : 2 * width], preferred_element_type=F32
+    ).astype(BF)
+    val[...] = jnp.dot(normed, wqkv[:, 2 * width :], preferred_element_type=F32).astype(BF)
+    tails = nbuf[:, width:]
     pick = jnp.where(
         lax.broadcasted_iota(jnp.int32, (8, LANES), 0)
         == lax.broadcasted_iota(jnp.int32, (8, LANES), 1),
@@ -258,6 +304,24 @@
     res_c = col_ints[1:2].astype(jnp.int32)
     valid = jnp.where(col_ints[2:3] == 1.0, 1.0, 0.0)
     class_ids = lax.broadcasted_iota(jnp.int32, (cpad, cols), 0)
+
+    emask = jnp.where(
+        lax.broadcasted_iota(jnp.int32, (heads, LANES), 0)
+        == lax.broadcasted_iota(jnp.int32, (heads, LANES), 1),
+        1.0,
+        0.0,
+    )
+
+    def exchange(p, k):
+        at = pl.ds(pl.multiple_of(k * NC, NC), NC)
+        return pltpu.make_async_remote_copy(
+            src_ref=nd.at[at],
+            dst_ref=xbuf.at[p - 1, at],
+            send_sem=xsend.at[p - 1, k],
+            recv_sem=xrecv.at[p - 1, k],
+            device_id={"col": lax.rem(c + p, ncol)},
+            device_id_type=MESH,
+        )
 
     def attend(k, carry):
         base = pl.multiple_of(k * NC, NC)
@@ -284,25 +348,12 @@
         full = jnp.dot(gated, val[...], preferred_element_type=F32)
         dsum = jnp.sum(weights, axis=1, keepdims=True)
         nd[pl.ds(base, NC), :width] = jnp.sum(full.reshape(NC, heads, width) * mask[None], axis=1)
-        nd[pl.ds(base, NC), width:] = jnp.sum(dsum.reshape(NC, heads, 1) * mask[None], axis=1)
+        nd[pl.ds(base, NC), width:] = jnp.sum(dsum.reshape(NC, heads, 1) * emask[None], axis=1)
+        for p in range(1, ncol):
+            exchange(p, k).start()
         return carry
 
     lax.fori_loop(0, rows // NC, attend, 0)
-
-    def exchange(p):
-        return pltpu.make_async_remote_copy(
-            src_ref=nd,
-            dst_ref=xbuf.at[p - 1],
-            send_sem=xsend.at[p - 1],
-            recv_sem=xrecv.at[p - 1],
-            device_id={"col": lax.rem(c + p, ncol)},
-            device_id_type=MESH,
-        )
-
-    for p in range(1, ncol):
-        exchange(p).start()
-
-    win = (0.5 * win_ref[...].astype(F32)).astype(BF)
 
     def mlp_block(b, carry):
         def chunk(k, carry):
@@ -317,7 +368,7 @@
                 ],
                 axis=1,
             )
-            first = z + jnp.dot(wedge_ref[...], lg, preferred_element_type=F32)
+            first = z + jnp.dot(wedge, lg, preferred_element_type=F32)
             enorm = chan_norm(first, egain)
             y = jnp.dot(win, enorm, preferred_element_type=F32)
             arg = y * (GELU_A + GELU_B * (y * y))
@@ -341,22 +392,32 @@
 
     total = nd[...]
     for p in range(1, ncol):
-        exchange(p).wait_recv()
+        for k in range(rows // NC):
+            exchange(p, k).wait_recv()
         total = total + xbuf[p - 1]
-    attended = (total[:, :width] / total[:, width:]).astype(BF)
+    expand = jnp.where(
+        lax.broadcasted_iota(jnp.int32, (LANES, width), 1) // hsize
+        == lax.broadcasted_iota(jnp.int32, (LANES, width), 0),
+        1.0,
+        0.0,
+    )
+    denom = jnp.dot(
+        total[:, width:],
+        expand,
+        precision=lax.Precision.HIGHEST,
+        preferred_element_type=F32,
+    )
+    attended = (total[:, :width] / denom).astype(BF)
     wo_copy.wait()
     node_out[...] = jnp.dot(attended, wo[...], preferred_element_type=F32).astype(BF)
 
     for p in range(1, ncol):
-        exchange(p).wait_send()
-
-    @pl.when(is_src)
-    def _():
-        for p in range(1, half):
-            direct(p).wait_send()
-
-    for k in range(npc // 2):
-        forward(k).wait_send()
+        for k in range(rows // NC):
+            exchange(p, k).wait_send()
+        across(p).wait_send()
+    for p in range(1, half):
+        direct(p).wait_send()
+    twin.wait_send()
     for b in range(nblk):
         pair_outc(b).wait()
 
@@ -386,14 +447,13 @@
     npc = cols // rows
     nblk = rows // IB
     nl = cols // LANES
-    ints = jnp.stack([chain_ids, residue_index, pad_mask], axis=0)
     vm = pl.BlockSpec(memory_space=pltpu.VMEM)
     sm = pl.BlockSpec(memory_space=pltpu.SMEM)
     hb = pl.BlockSpec(memory_space=pl.ANY)
     dma = pltpu.SemaphoreType.DMA
     return pl.pallas_call(
         functools.partial(fused_kernel, nrow, ncol),
-        in_specs=[sm, sm, vm, vm, hb, hb, hb] + [vm] * 8,
+        in_specs=[sm, sm, vm, vm, vm, vm, hb, hb, hb] + [vm] * 8,
         out_specs=[vm, hb],
         out_shape=[
             jax.ShapeDtypeStruct((rows, width), BF),
@@ -401,7 +461,10 @@
         ],
         scratch_shapes=[
             pltpu.VMEM((rows, width + LANES), BF),
-            pltpu.VMEM((npc, rows, width + LANES), BF),
+            pltpu.VMEM((nrow // 2, rows // ncol, width + LANES), BF),
+            pltpu.VMEM((ncol, npc // 2, rows // ncol, width + LANES), BF),
+            pltpu.VMEM((ncol, npc // 2, rows // ncol, width + LANES), BF),
+            pltpu.VMEM((cols, width + LANES), BF),
             pltpu.VMEM(w_qkv.shape, BF),
             pltpu.VMEM(w_out.shape, BF),
             pltpu.VMEM((nblk, chans, IB, cols), BF),
@@ -415,16 +478,18 @@
             pltpu.VMEM((cols, width), BF),
             pltpu.VMEM((cols, width), BF),
             pltpu.VMEM((NC * heads, width), BF),
-            pltpu.VMEM((rows, 2 * width), F32),
-            pltpu.VMEM((ncol - 1, rows, 2 * width), F32),
+            pltpu.VMEM((rows, width + LANES), F32),
+            pltpu.VMEM((ncol - 1, rows, width + LANES), F32),
             dma((nblk,)),
             dma((nblk,)),
             dma((2,)),
             dma((nrow // 2,)),
-            dma((npc // 2,)),
-            dma((npc,)),
-            dma((ncol - 1,)),
-            dma((ncol - 1,)),
+            dma((nrow // 2,)),
+            dma((ncol,)),
+            dma((ncol,)),
+            dma((2,)),
+            dma((ncol - 1, rows // NC)),
+            dma((ncol - 1, rows // NC)),
         ],
         compiler_params=pltpu.CompilerParams(
             vmem_limit_bytes=60 << 20, collective_id=0, has_side_effects=True
@@ -433,18 +498,20 @@
     )(
         chain_ids,
         residue_index,
-        ints,
+        chain_ids[None],
+        residue_index[None],
+        pad_mask[None],
         nodes,
         pairs,
         w_qkv,
         w_out,
-        node_gain[None],
+        node_gain.reshape(width // LANES, LANES),
         pair_gain[None],
         edge_norm_gain[None],
-        w_bias_gate,
+        w_bias_gate.T,
         rel_table,
-        w_edge,
-        w_mlp_in,
+        w_edge.T,
+        w_mlp_in.T,
         w_mlp_out,
     )
 

time: 52.9 us -> 45.3 us (0.86)
  the two profiles are of different devices: /device:TPU:14 before, /device:TPU:1 now
where the time goes in v3:
time: 45.3 us; the launch traced here: 45.1 us
  Pallas kernels  39.8 us (88%)
  local copies, waits for them, and re-layouts  4.7 us (10%)
  between operations  0.64 us (1%)
    pallas_call x1, Pallas kernels, body(): pl.pallas_call(functools.partial(fused_kernel, nrow, ncol), in_specs=[sm,...  39.8 us
    unnamed x2, local copies, waits for them, and re-layouts  4.7 us

profile of v3, /device:TPU:1, one launch (start us, length us, event | category | flops | bytes accessed | tf_op | source)
XLA Modules:
  0.0 45.1 jit_solution(699307202041307697)
XLA Ops:
  0.6 39.8 %fused_layer.1 = (bf16[64,768]{1,0:T(8,128)(2,1)}, bf16[64,64,256]{2,1,0:T(8,128)(2,1)}) custom-call(s32[64]{0:T(128)} %chain_s.1, s32[64]{0:T(128)} %res_s.1, s32[1,64]{1,0:T(1,128)} %bitcast.13, s32[1,64]{1,0:T(1,128)} %bitcast.14, s32[1,64]{1,0:T(1,128)} %bitcast.15, bf16[64,768]{1,0:T(8,128)(2,1)} %nodes_ref.1, bf16[64,64,256]{2,1,0:T(8,128)(2,1)} %pairs_hbm.1, ...), custom_call_target="tpu_custom_call" | custom-call | tf_op jit(solution)/shard_map/fused_layer/pallas_call | solution.py:454
  40.4 1.5 %copy.19 = bf16[64,768]{1,0:T(8,128)(2,1)} copy(bf16[64,768]{1,0:T(8,128)(2,1)} %get-tuple-element.4) | data formatting | bytes 196608
  42.0 3.2 %copy.20 = bf16[64,64,256]{2,1,0:T(8,128)(2,1)} copy(bf16[64,64,256]{2,1,0:T(8,128)(2,1)} %get-tuple-element.5) | data formatting | bytes 4194304

commit v4 on v3

--- a/solution.py
+++ b/solution.py
@@ -7,9 +7,9 @@
 from jax.sharding import PartitionSpec as P
 
 IB = 16
-NA = 4
+NA = 8
 NC = 8
-ND = 4
+ND = 8
 GELU_A = 2.0 * (2.0 / 3.141592653589793) ** 0.5
 GELU_B = GELU_A * 4.0 * 0.044715
 MESH = pl.DeviceIdType.MESH
@@ -153,7 +153,6 @@
     for k, ref in enumerate((chain_ref, res_ref, pad_ref)):
         tail = jnp.where(lane == k, column(ref[...].astype(F32)), tail)
     snd[:, width:] = tail.astype(BF)
-    pl.semaphore_wait(barrier, half + ncol - 1)
 
     def direct(p):
         peer = lax.rem(chip + p, half) * 2 + par
@@ -209,9 +208,9 @@
     )
 
     gbuf[chip] = snd[pl.ds(pl.multiple_of(c * prow, prow), prow), :]
+    pl.semaphore_wait(barrier, half + ncol - 1)
     for p in range(1, half):
         direct(p).start()
-
     mask = jnp.where(
         lax.broadcasted_iota(jnp.int32, (heads, width), 1) // hsize
         == lax.broadcasted_iota(jnp.int32, (heads, width), 0),
@@ -265,6 +264,10 @@
 
     for b in range(nblk - 1):
         bias_block(b)
+    wq_copy.wait()
+    own = node_norm(nodes_ref[...].astype(F32), ngain)
+    query = jnp.dot(own, wqkv[:, :width], preferred_element_type=F32)
+    qf[...] = 0.25 * query.astype(BF).astype(F32)
     for p in range(1, half):
         direct_in(p).wait_recv()
     for p in range(1, ncol):
@@ -274,10 +277,6 @@
     for p in range(1, ncol):
         across_in(p).wait_recv()
     twin.start()
-    wq_copy.wait()
-    own = node_norm(nodes_ref[...].astype(F32), ngain)
-    query = jnp.dot(own, wqkv[:, :width], preferred_element_type=F32)
-    qf[...] = 0.25 * query.astype(BF).astype(F32)
     twin.wait_recv()
     for k in range(h2):
         for q in range(ncol):

time: 45.3 us -> 42.2 us (0.932)
  Pallas kernels: 39.8 us -> 36.7 us
    pallas_call x1, Pallas kernels: 39.8 us -> 36.7 us  [body(): pl.pallas_call(functools.partial(fused_kernel, nrow, ncol), in_specs=[sm,...]
where the time goes in v4:
time: 42.2 us; the launch traced here: 42 us
  Pallas kernels  36.7 us (87%)
  local copies, waits for them, and re-layouts  4.7 us (11%)
  between operations  0.64 us (2%)
    pallas_call x1, Pallas kernels, body(): pl.pallas_call(functools.partial(fused_kernel, nrow, ncol), in_specs=[sm,...  36.7 us
    unnamed x2, local copies, waits for them, and re-layouts  4.7 us

profile of v4, /device:TPU:1, one launch (start us, length us, event | category | flops | bytes accessed | tf_op | source)
XLA Modules:
  0.0 42.0 jit_solution(1354897751984084737)
XLA Ops:
  0.6 36.7 %fused_layer.1 = (bf16[64,768]{1,0:T(8,128)(2,1)}, bf16[64,64,256]{2,1,0:T(8,128)(2,1)}) custom-call(s32[64]{0:T(128)} %chain_s.1, s32[64]{0:T(128)} %res_s.1, s32[1,64]{1,0:T(1,128)} %bitcast.13, s32[1,64]{1,0:T(1,128)} %bitcast.14, s32[1,64]{1,0:T(1,128)} %bitcast.15, bf16[64,768]{1,0:T(8,128)(2,1)} %nodes_ref.1, bf16[64,64,256]{2,1,0:T(8,128)(2,1)} %pairs_hbm.1, ...), custom_call_target="tpu_custom_call" | custom-call | tf_op jit(solution)/shard_map/fused_layer/pallas_call | solution.py:453
  37.3 1.5 %copy.19 = bf16[64,768]{1,0:T(8,128)(2,1)} copy(bf16[64,768]{1,0:T(8,128)(2,1)} %get-tuple-element.4) | data formatting | bytes 196608
  38.9 3.2 %copy.20 = bf16[64,64,256]{2,1,0:T(8,128)(2,1)} copy(bf16[64,64,256]{2,1,0:T(8,128)(2,1)} %get-tuple-element.5) | data formatting | bytes 4194304

commit v5 on v4

--- a/solution.py
+++ b/solution.py
@@ -8,7 +8,7 @@
 
 IB = 16
 NA = 8
-NC = 8
+NC = 16
 ND = 8
 GELU_A = 2.0 * (2.0 / 3.141592653589793) ** 0.5
 GELU_B = GELU_A * 4.0 * 0.044715

time: 42.2 us -> 41.2 us (0.976)
  Pallas kernels: 36.7 us -> 35.6 us
    pallas_call x1, Pallas kernels: 36.7 us -> 35.6 us  [body(): pl.pallas_call(functools.partial(fused_kernel, nrow, ncol), in_specs=[sm,...]
where the time goes in v5:
time: 41.2 us; the launch traced here: 40.9 us
  Pallas kernels  35.6 us (86%)
  local copies, waits for them, and re-layouts  4.7 us (11%)
  between operations  0.64 us (2%)
    pallas_call x1, Pallas kernels, body(): pl.pallas_call(functools.partial(fused_kernel, nrow, ncol), in_specs=[sm,...  35.6 us
    unnamed x2, local copies, waits for them, and re-layouts  4.7 us

profile of v5, /device:TPU:1, one launch (start us, length us, event | category | flops | bytes accessed | tf_op | source)
XLA Modules:
  0.0 40.9 jit_solution(16647656824087034493)
XLA Ops:
  0.6 35.6 %fused_layer.1 = (bf16[64,768]{1,0:T(8,128)(2,1)}, bf16[64,64,256]{2,1,0:T(8,128)(2,1)}) custom-call(s32[64]{0:T(128)} %chain_s.1, s32[64]{0:T(128)} %res_s.1, s32[1,64]{1,0:T(1,128)} %bitcast.13, s32[1,64]{1,0:T(1,128)} %bitcast.14, s32[1,64]{1,0:T(1,128)} %bitcast.15, bf16[64,768]{1,0:T(8,128)(2,1)} %nodes_ref.1, bf16[64,64,256]{2,1,0:T(8,128)(2,1)} %pairs_hbm.1, ...), custom_call_target="tpu_custom_call" | custom-call | tf_op jit(solution)/shard_map/fused_layer/pallas_call | solution.py:453
  36.2 1.5 %copy.19 = bf16[64,768]{1,0:T(8,128)(2,1)} copy(bf16[64,768]{1,0:T(8,128)(2,1)} %get-tuple-element.4) | data formatting | bytes 196608
  37.8 3.2 %copy.20 = bf16[64,64,256]{2,1,0:T(8,128)(2,1)} copy(bf16[64,64,256]{2,1,0:T(8,128)(2,1)} %get-tuple-element.5) | data formatting | bytes 4194304
